TPU v7x, 32 devices: a whole 2x2x4 slice. The times are simulated.
32 devices in a mesh: vol: 16 (over z, x, core), slab: 2 (over y).
Axes of the slice: x: 2, y: 2, z: 4, core: 2. Of those that a mesh axis runs over, the one named last changes fastest.
Arguments:
- volumes: bfloat16 [32, 4, 16, 16, 64], P('vol', None, 'slab'), may hold values from -6 to 6
- w_first: bfloat16 [32, 108], replicated, may hold values from -0.625 to 0.625
- w_second: bfloat16 [64, 864], replicated, may hold values from -0.21875 to 0.21875
- w_third: bfloat16 [128, 1728], replicated, may hold values from -0.15625 to 0.15625
- map_grad: bfloat16 [32, 128, 4, 4, 16], P(('vol', 'slab')), may hold values from -6 to 6
Outputs:
- grad_first: float32 [32, 108], replicated
- grad_second: float32 [64, 864], replicated
- grad_third: float32 [128, 1728], replicated
All inputs are finite; a program needn't handle non-finite values.
Results may differ from a plain program's by a relative error of at most 0.0071.
Values may be sent and summed in bfloat16 or wider, within the bound.
A program may use at most 64 MiB of HBM per device.

v0:
```python
import jax
import jax.numpy as jnp
from jax import lax
from jax.sharding import PartitionSpec as P

FORWARD_DIMS = ("NCDHW", "OIDHW", "NCDHW")
FILTER_DIMS = ("CNDHW", "IODHW", "CNDHW")
SPREAD_DIMS = ("NCDHW", "IODHW", "NCDHW")


def shifted(array, axis, by):
    length = lax.axis_size(axis)
    pairs = [(i, i + by) for i in range(length) if 0 <= i + by < length]
    return lax.ppermute(array, axis, pairs)


def kernel_of(weight):
    channels = weight.shape[1] // 27
    return weight.reshape(weight.shape[0], 3, 3, 3, channels).transpose(0, 4, 1, 2, 3)


def flat_of(kernel):
    return kernel.transpose(0, 2, 3, 4, 1).reshape(kernel.shape[0], -1)


def forward(maps, weight, stride, pads):
    return lax.conv_general_dilated(
        maps,
        kernel_of(weight),
        (stride, stride, stride),
        pads,
        dimension_numbers=FORWARD_DIMS,
        preferred_element_type=jnp.float32,
    )


def weight_grad(maps, delta, stride, pads):
    bounds = []
    for dim_index in range(3):
        extent = maps.shape[2 + dim_index]
        lower = pads[dim_index][0]
        cells_out = delta.shape[2 + dim_index]
        bounds.append((lower, 3 - extent - lower + (cells_out - 1) * stride))
    kernel = lax.conv_general_dilated(
        maps,
        delta,
        (1, 1, 1),
        bounds,
        rhs_dilation=(stride, stride, stride),
        dimension_numbers=FILTER_DIMS,
        preferred_element_type=jnp.float32,
    )
    return flat_of(kernel)


def spread_back(delta, weight, stride):
    kernel = kernel_of(weight)[:, :, ::-1, ::-1, ::-1]
    return lax.conv_general_dilated(
        delta,
        kernel,
        (1, 1, 1),
        ((2, 2), (2, 2), (2, 2)),
        lhs_dilation=(stride, stride, stride),
        dimension_numbers=SPREAD_DIMS,
        preferred_element_type=jnp.float32,
    )


def interior(full, shape):
    return full[:, :, 1 : 1 + shape[2], 1 : 1 + shape[3], 1 : 1 + shape[4]]


def silu_slope(pre):
    sigma = jax.nn.sigmoid(pre)
    return sigma * (1.0 + pre * (1.0 - sigma))


def per_device(volumes, w_first, w_second, w_third, map_grad):
    full_pads = ((1, 1), (1, 1), (1, 1))
    slab_pads = ((0, 0), (1, 1), (1, 1))
    lower_rim = shifted(volumes[:, :, -1:], "slab", 1)
    first_in = jnp.concatenate([lower_rim, volumes], axis=2)
    pre_first = forward(first_in, w_first, 2, slab_pads)
    act_first = jax.nn.silu(pre_first).astype(jnp.bfloat16)
    lower_maps = shifted(act_first[:, :, -1:], "slab", 1)
    second_in = jnp.concatenate([lower_maps, act_first], axis=2)
    pre_second = forward(second_in, w_second, 2, slab_pads)
    act_second = jax.nn.silu(pre_second).astype(jnp.bfloat16)
    sample_maps = lax.all_to_all(act_second, "slab", split_axis=0, concat_axis=2, tiled=True)
    pre_third = forward(sample_maps, w_third, 1, full_pads)
    delta_third = (map_grad.astype(jnp.float32) * silu_slope(pre_third)).astype(jnp.bfloat16)
    grad_third = weight_grad(sample_maps, delta_third, 1, full_pads)
    back_second = interior(spread_back(delta_third, w_third, 1), sample_maps.shape).astype(
        jnp.bfloat16
    )
    back_second = lax.all_to_all(back_second, "slab", split_axis=2, concat_axis=0, tiled=True)
    delta_second = (back_second.astype(jnp.float32) * silu_slope(pre_second)).astype(jnp.bfloat16)
    grad_second = weight_grad(second_in, delta_second, 2, slab_pads)
    upper_rim = shifted(delta_second[:, :, :1], "slab", -1)
    extended = jnp.concatenate([delta_second, upper_rim], axis=2)
    back_first = interior(spread_back(extended, w_second, 2), act_first.shape)
    delta_first = (back_first * silu_slope(pre_first)).astype(jnp.bfloat16)
    grad_first = weight_grad(first_in, delta_first, 2, slab_pads)
    grad_first, grad_second, grad_third = lax.psum(
        (grad_first, grad_second, grad_third), ("vol", "slab")
    )
    factor = 1.0 / (map_grad.shape[0] * lax.axis_size("vol") * lax.axis_size("slab"))
    return (grad_first * factor, grad_second * factor, grad_third * factor)


def solution(mesh):
    return jax.shard_map(
        per_device,
        mesh=mesh,
        in_specs=(
            P("vol", None, "slab", None, None),
            P(),
            P(),
            P(),
            P(("vol", "slab"), None, None, None, None),
        ),
        out_specs=(P(), P(), P()),
        check_vma=False,
    )
```

profile of v0, /device:TPU:0, one launch (start us, length us, event | category | flops | bytes accessed | tf_op | source)
XLA Modules:
  0.0 215.7 jit_solution(3907313156765782653)
XLA Ops:
  7.2 0.8 slice.15
  8.0 4.9 %collective-permute-start = (bf16[2,4,1,16,64]{4,3,2,1,0:T(8,128)(2,1)S(1)}, bf16[2,4,1,16,64]{4,3,2,1,0:T(8,128)(2,1)S(1)}, u32[]{:S(2)}, u32[]{:S(2)}) collective-permute-start(bf16[2,4,1,16,64]{4,3,2,1,0:T(8,128)(2,1)S(1)} %slice.15), channel_id=1, source_target_pairs={{0,1},{2,3},{4,5},{6,7},{8,9},{10,11},{12,13},{14,15},{16,17},{18,... | collective-permute-start | bytes 49160 | tf_op jit(solution)/shard_map/ppermute | solution.py:14
  12.9 0.8 copy.132
  13.7 0.7 collective-permute-done
  14.5 1.0 constant_dynamic-update-slice_fusion
  15.5 0.2 pad.clone
  15.6 1.5 reshape.38
  17.2 0.7 slice.34
  17.9 3.0 %fusion.2 = bf16[4,9,16,2,8,12]{5,4,2,3,1,0:T(8,128)(2,1)} fusion(bf16[4,9,16,2,7,2]{5,4,2,3,1,0:T(8,128)(2,1)S(1)} %slice.34, bf16[4,9,16,2,8,10]{5,4,2,3,1,0:T(8,128)(2,1)S(1)} %reshape.38), kind=kLoop, calls=%fused_computation.4 | loop fusion | flops 663552 | bytes 437760 | tf_op jit(solution)/shard_map/conv_general_dilated | solution.py:27
  20.9 5.2 %copy.131 = bf16[4,9,16,2,8,12]{2,4,3,5,1,0:T(8,128)(2,1)S(1)} copy(bf16[4,9,16,2,8,12]{5,4,2,3,1,0:T(8,128)(2,1)} %fusion.2) | data formatting | bytes 442368 | tf_op jit(solution)/shard_map/conv_general_dilated | solution.py:27
  26.1 2.4 %copy.133 = bf16[4,9,16,16,12]{3,0,4,2,1:T(4,128)(2,1)} copy(bf16[4,9,16,16,12]{2,3,4,1,0:T(8,128)(2,1)S(1)} %bitcast.102) | data formatting | bytes 442368 | tf_op jit(solution)/shard_map/conv_general_dilated | solution.py:27
  28.5 4.7 %multiply_convert_fusion = (bf16[4,8,16,5,32]{4,2,3,1,0:T(8,128)(2,1)S(1)}, f32[4,8,16,5,32]{4,2,3,1,0:T(8,128)}) fusion(bf16[4,9,16,16,12]{3,0,4,2,1:T(4,128)(2,1)} %copy.133, bf16[32,3,3,3,4]{0,4,3,2,1:T(4,128)(2,1)S(1)} %reshape.30, pred[16,5]{0,1:T(8,128)(4,1)S(1)} %copy-done.5), kind=kOutput, calls=%fused_computation.14 | convolution fusion | flops 17776640 | bytes 719696 | tf_op jit(solution)/shard_map/conv_general_dilated | solution.py:27
  33.4 0.1 copy.194
  33.5 4.2 %collective-permute-start.1 = (bf16[2,32,1,8,32]{1,0,4,3,2:T(2,128)(2,1)S(1)}, bf16[2,32,1,8,32]{1,0,4,3,2:T(2,128)(2,1)S(1)}, u32[]{:S(2)}, u32[]{:S(2)}) collective-permute-start(bf16[2,32,1,8,32]{1,0,4,3,2:T(2,128)(2,1)S(1)} %bitcast.129), channel_id=1, source_target_pairs={{0,1},{2,3},{4,5},{6,7},{8,9},{10,11},{12,13},{14,15},{16,17},{18,... | collective-permute-start | bytes 98312 | tf_op jit(solution)/shard_map/ppermute | solution.py:14
  37.7 0.2 copy.140
  37.9 0.2 copy.136
  38.1 0.5 copy.193
  38.7 1.5 collective-permute-done.1
  40.2 1.0 fusion.55
  41.2 0.9 pad.2
  42.1 0.2 copy.139
  42.5 0.3 copy-done.7
  42.8 0.8 multiply_convert_fusion.1
  43.7 0.7 reshape.100
  44.5 3.7 %all-to-all-start = ((bf16[2,2,4096]{2,1,0:T(2,128)(2,1)}), bf16[2,2,4096]{2,1,0:T(2,128)(2,1)S(1)}, u32[]{:S(2)}, u32[]{:S(2)}) async-start(bf16[2,2,4096]{2,1,0:T(2,128)(2,1)} %reshape.100), calls=%async_computation | async-start | bytes 65536 | tf_op jit(solution)/shard_map/all_to_all | solution.py:89
  48.2 8.7 %copy.159 = bf16[2,4,9,16,64]{1,0,4,3,2:T(2,128)(2,1)} copy(bf16[2,4,9,16,64]{4,3,2,1,0:T(8,128)(2,1)S(1)} %constant_dynamic-update-slice_fusion) | data formatting | bytes 294912 | tf_op jit(solution)/shard_map/concatenate | solution.py:82
  56.8 1.7 copy.158
  58.7 0.1 reshape.101
  59.0 0.6 add_multiply_fusion.1
  59.8 0.8 fusion.10
  60.7 0.7 reshape.102
  61.5 3.5 %all-to-all-start.1 = ((bf16[2,2,4096]{2,1,0:T(2,128)(2,1)}), bf16[2,2,4096]{2,1,0:T(2,128)(2,1)S(1)}, u32[]{:S(2)}, u32[]{:S(2)}) async-start(bf16[2,2,4096]{2,1,0:T(2,128)(2,1)} %reshape.102), calls=%async_computation.1 | async-start | bytes 65536 | tf_op jit(solution)/shard_map/all_to_all | solution.py:96
  64.9 2.5 %fusion.39 = f32[128,3,3,3,64]{0,4,3,2,1:T(8,128)} fusion(bf16[1,128,4,4,16]{1,3,4,2,0:T(4,128)(2,1)S(1)} %fusion.36, bf16[1,64,4,4,16]{1,4,3,2,0:T(8,128)(2,1)S(1)} %bitcast.112), kind=kOutput, calls=%fused_computation.57 | convolution fusion | flops 75366400 | bytes 983040 | tf_op jit(solution)/shard_map/transpose | solution.py:23
  67.5 1.4 all-to-all-done.1
  69.1 1.3 collective-permute-start.2
  70.4 1.6 fusion.44
  72.0 0.9 copy.162
  72.8 2.0 collective-permute-done.2
  75.0 0.1 pad.8.clone
  75.2 0.2 fusion.20
  75.4 0.8 convolution_select_fusion
  76.3 0.9 copy.157
  77.3 11.5 %fusion.16 = f32[32,3,3,3,4]{0,4,3,2,1:T(4,128)S(1)} fusion(bf16[2,4,9,16,64]{1,0,4,3,2:T(2,128)(2,1)} %copy.159, bf16[4,8,2,32,32]{4,1,3,2,0:T(8,128)(2,1)S(1)} %fusion.14), kind=kOutput, calls=%fused_computation.26 | convolution fusion | flops 13424640 | bytes 292352 | tf_op jit(solution)/shard_map/transpose | solution.py:23
  88.9 40.4 %psum.21 = f32[32,108]{0,1:T(8,128)S(1)} all-reduce(f32[32,108]{0,1:T(8,128)S(1)} %reshape.33), channel_id=1, replica_groups=mesh['vol'=16,'slab'=2] {'vol','slab'}, use_global_device_ids=true, to_apply=%region_0.1 | all-reduce | flops 3456 | bytes 27648 | tf_op jit(solution)/shard_map/psum | solution.py:104
  129.2 0.7 copy.165
  129.9 76.0 %all-reduce.3.cloned.1.call-done = (f32[64,864]{1,0:T(8,128)}, f32[128,1728]{0,1:T(8,128)}) async-done(((f32[64,864]{1,0:T(8,128)}, f32[128,1728]{0,1:T(8,128)}), (f32[64,864]{1,0:T(8,128)}, f32[128,1728]{0,1:T(8,128)})) %all-reduce.3.cloned.1.call-update) | async-done | bytes 1105936 | tf_op jit(solution)/shard_map/psum | solution.py:104
  206.0 2.2 %broadcast_multiply_fusion = f32[128,1728]{0,1:T(8,128)} fusion(f32[128,1728]{0,1:T(8,128)} %get-tuple-element.16), kind=kLoop, calls=%fused_computation.28 | loop fusion | flops 221184 | bytes 1769472 | tf_op jit(solution)/shard_map/mul | solution.py:108
  208.1 0.7 broadcast_multiply_fusion.1
  (52 shorter events, 1.2 us)
Async XLA Ops:
  7.2 51.8 %copy-start = (bf16[128,1728]{0,1:T(8,128)(2,1)S(1)}, bf16[128,1728]{0,1:T(8,128)(2,1)}, u32[]{:S(2)}) copy-start(bf16[128,1728]{0,1:T(8,128)(2,1)} %param.8) | copy-start | bytes 1327108
  8.0 6.4 %collective-permute-start = (bf16[2,4,1,16,64]{4,3,2,1,0:T(8,128)(2,1)S(1)}, bf16[2,4,1,16,64]{4,3,2,1,0:T(8,128)(2,1)S(1)}, u32[]{:S(2)}, u32[]{:S(2)}) collective-permute-start(bf16[2,4,1,16,64]{4,3,2,1,0:T(8,128)(2,1)S(1)} %slice.15), channel_id=1, source_target_pairs={{0,1},{2,3},{4,5},{6,7},{8,9},{10,11},{12,13},{14,15},{16,17},{18,... | collective-permute-start | bytes 49160 | tf_op jit(solution)/shard_map/ppermute | solution.py:14
  26.1 2.4 %copy-start.5 = (pred[16,5]{0,1:T(8,128)(4,1)S(1)}, pred[16,5]{0,1:T(8,128)(4,1)}, u32[]{:S(2)}) copy-start(pred[16,5]{0,1:T(8,128)(4,1)} %constant.38) | copy-start | bytes 244
  28.5 9.2 %copy-start.2 = (bf16[64,864]{1,0:T(8,128)(2,1)S(1)}, bf16[64,864]{1,0:T(8,128)(2,1)}, u32[]{:S(2)}) copy-start(bf16[64,864]{1,0:T(8,128)(2,1)} %param.7) | copy-start | bytes 331780
  33.5 6.7 %collective-permute-start.1 = (bf16[2,32,1,8,32]{1,0,4,3,2:T(2,128)(2,1)S(1)}, bf16[2,32,1,8,32]{1,0,4,3,2:T(2,128)(2,1)S(1)}, u32[]{:S(2)}, u32[]{:S(2)}) collective-permute-start(bf16[2,32,1,8,32]{1,0,4,3,2:T(2,128)(2,1)S(1)} %bitcast.129), channel_id=1, source_target_pairs={{0,1},{2,3},{4,5},{6,7},{8,9},{10,11},{12,13},{14,15},{16,17},{18,... | collective-permute-start | bytes 98312 | tf_op jit(solution)/shard_map/ppermute | solution.py:14
  42.1 0.7 copy-start.7
  44.5 14.2 %all-to-all-start = ((bf16[2,2,4096]{2,1,0:T(2,128)(2,1)}), bf16[2,2,4096]{2,1,0:T(2,128)(2,1)S(1)}, u32[]{:S(2)}, u32[]{:S(2)}) async-start(bf16[2,2,4096]{2,1,0:T(2,128)(2,1)} %reshape.100), calls=%async_computation | async-start | bytes 65536 | tf_op jit(solution)/shard_map/all_to_all | solution.py:89
  56.8 2.1 copy-start.6
  58.7 1.0 copy-start.3
  61.5 7.4 %all-to-all-start.1 = ((bf16[2,2,4096]{2,1,0:T(2,128)(2,1)}), bf16[2,2,4096]{2,1,0:T(2,128)(2,1)S(1)}, u32[]{:S(2)}, u32[]{:S(2)}) async-start(bf16[2,2,4096]{2,1,0:T(2,128)(2,1)} %reshape.102), calls=%async_computation.1 | async-start | bytes 65536 | tf_op jit(solution)/shard_map/all_to_all | solution.py:96
  64.9 141.0 %all-reduce.3.cloned.1.call-start = ((), (), s32[]{:S(2)}) async-start(), calls=%async_computation.2 | async-start | bytes 2228224 | tf_op jit(solution)/shard_map/psum | solution.py:104
  69.1 5.8 %collective-permute-start.2 = (bf16[2,64,1,4,16]{1,4,3,2,0:T(8,128)(2,1)S(1)}, bf16[2,64,1,4,16]{1,4,3,2,0:T(8,128)(2,1)S(1)}, u32[]{:S(2)}, u32[]{:S(2)}) collective-permute-start(bf16[2,64,1,4,16]{1,4,3,2,0:T(8,128)(2,1)S(1)} %slice.45), channel_id=1, source_target_pairs={{1,0},{3,2},{5,4},{7,6},{9,8},{11,10},{13,12},{15,14},{17,16},{19,... | collective-permute-start | bytes 49160 | tf_op jit(solution)/shard_map/ppermute | solution.py:14
  71.9 3.5 %copy-start.4 = (pred[16,6]{0,1:T(8,128)(4,1)S(1)}, pred[16,6]{0,1:T(8,128)(4,1)}, u32[]{:S(2)}) copy-start(pred[16,6]{0,1:T(8,128)(4,1)} %constant.34) | copy-start | bytes 292
  206.0 2.2 %copy-start.1 = (f32[64,864]{1,0:T(8,128)S(1)}, f32[64,864]{1,0:T(8,128)}, u32[]{:S(2)}) copy-start(f32[64,864]{1,0:T(8,128)} %get-tuple-element.15) | copy-start | bytes 663556
Sparse Core Ops, SparseCore 0:
  73.0 132.9 all-reduce.2
where the time goes:
time: 216 us
  waiting for transfers between devices  81.7 us (38%)
  blocking collectives  40.4 us (19%)
  local copies, waits for them, and re-layouts  30.6 us (14%)
  matrix products  23.5 us (11%)
  starting transfers between devices  17.6 us (8%)
  between operations  14.5 us (7%)
  other arithmetic  7.37 us (3%)
    psum x1, waiting for transfers between devices, per_device(): lax.psum((grad_first, grad_second, grad_third), ('vol', 'slab'))  76 us
    psum x1, blocking collectives, per_device(): lax.psum((grad_first, grad_second, grad_third), ('vol', 'slab'))  40.4 us
    transpose x3, matrix products, flat_of(): return kernel.transpose(0, 2, 3, 4, 1).reshape(kernel.shape[0], -1)  15.6 us
    ppermute x3, starting transfers between devices, shifted(): return lax.ppermute(array, axis, pairs)  10.4 us
    conv_general_dilated x8, local copies, waits for them, and re-layouts, forward(): lax.conv_general_dilated(maps, kernel_of(weight), (stride, stride, stride...  10.1 us
    concatenate x3, local copies, waits for them, and re-layouts, per_device(): first_in = jnp.concatenate([lower_rim, volumes], axis=2)  9.8 us
    conv_general_dilated x3, matrix products, forward(): lax.conv_general_dilated(maps, kernel_of(weight), (stride, stride, stride...  6.18 us
    unnamed x31, local copies, waits for them, and re-layouts  4.63 us
  transfers between devices with their start and end apart: 6, of which 5 were waited for; matrix products, arithmetic and copies ran while one was open for 15% of the time, Pallas kernels for 0%

commit v1 on v0

--- a/solution.py
+++ b/solution.py
@@ -93,7 +93,12 @@
     back_second = interior(spread_back(delta_third, w_third, 1), sample_maps.shape).astype(
         jnp.bfloat16
     )
-    back_second = lax.all_to_all(back_second, "slab", split_axis=2, concat_axis=0, tiled=True)
+    back_second = jnp.concatenate(
+        lax.all_to_all(
+            jnp.stack(jnp.split(back_second, lax.axis_size("slab"), axis=2)), "slab", 0, 0
+        ),
+        axis=0,
+    )
     delta_second = (back_second.astype(jnp.float32) * silu_slope(pre_second)).astype(jnp.bfloat16)
     grad_second = weight_grad(second_in, delta_second, 2, slab_pads)
     upper_rim = shifted(delta_second[:, :, :1], "slab", -1)

time: 216 us -> 216 us (level)
    unnamed x31 -> x30, local copies, waits for them, and re-layouts: 4.63 us -> 4.6 us
where the time goes in v1:
time: 216 us
  waiting for transfers between devices  81.7 us (38%)
  blocking collectives  40.3 us (19%)
  local copies, waits for them, and re-layouts  30.6 us (14%)
  matrix products  23.5 us (11%)
  starting transfers between devices  17.6 us (8%)
  between operations  14.6 us (7%)
  other arithmetic  7.38 us (3%)
    psum x1, waiting for transfers between devices, per_device(): lax.psum((grad_first, grad_second, grad_third), ('vol', 'slab'))  76 us
    psum x1, blocking collectives, per_device(): lax.psum((grad_first, grad_second, grad_third), ('vol', 'slab'))  40.3 us
    transpose x3, matrix products, flat_of(): return kernel.transpose(0, 2, 3, 4, 1).reshape(kernel.shape[0], -1)  15.6 us
    ppermute x3, starting transfers between devices, shifted(): return lax.ppermute(array, axis, pairs)  10.4 us
    conv_general_dilated x8, local copies, waits for them, and re-layouts, forward(): lax.conv_general_dilated(maps, kernel_of(weight), (stride, stride, stride...  10.1 us
    concatenate x3, local copies, waits for them, and re-layouts, per_device(): first_in = jnp.concatenate([lower_rim, volumes], axis=2)  9.76 us
    conv_general_dilated x3, matrix products, forward(): lax.conv_general_dilated(maps, kernel_of(weight), (stride, stride, stride...  6.17 us
    unnamed x30, local copies, waits for them, and re-layouts  4.6 us
  transfers between devices with their start and end apart: 6, of which 5 were waited for; matrix products, arithmetic and copies ran while one was open for 15% of the time, Pallas kernels for 0%

profile of v1, /device:TPU:0, one launch (start us, length us, event | category | flops | bytes accessed | tf_op | source)
XLA Modules:
  0.0 215.6 jit_solution(8688615663429315844)
XLA Ops:
  7.2 0.8 slice.15
  8.0 4.9 %collective-permute-start = (bf16[2,4,1,16,64]{4,3,2,1,0:T(8,128)(2,1)S(1)}, bf16[2,4,1,16,64]{4,3,2,1,0:T(8,128)(2,1)S(1)}, u32[]{:S(2)}, u32[]{:S(2)}) collective-permute-start(bf16[2,4,1,16,64]{4,3,2,1,0:T(8,128)(2,1)S(1)} %slice.15), channel_id=1, source_target_pairs={{0,1},{2,3},{4,5},{6,7},{8,9},{10,11},{12,13},{14,15},{16,17},{18,... | collective-permute-start | bytes 49160 | tf_op jit(solution)/shard_map/ppermute | solution.py:14
  12.9 0.8 copy.137
  13.7 0.7 collective-permute-done
  14.5 1.0 constant_dynamic-update-slice_fusion
  15.5 0.2 pad.clone
  15.6 1.5 reshape.37
  17.2 0.7 slice.37
  17.9 3.0 %fusion.2 = bf16[4,9,16,2,8,12]{5,4,2,3,1,0:T(8,128)(2,1)} fusion(bf16[4,9,16,2,7,2]{5,4,2,3,1,0:T(8,128)(2,1)S(1)} %slice.37, bf16[4,9,16,2,8,10]{5,4,2,3,1,0:T(8,128)(2,1)S(1)} %reshape.37), kind=kLoop, calls=%fused_computation.4 | loop fusion | flops 663552 | bytes 437760 | tf_op jit(solution)/shard_map/conv_general_dilated | solution.py:27
  20.9 5.2 %copy.136 = bf16[4,9,16,2,8,12]{2,4,3,5,1,0:T(8,128)(2,1)S(1)} copy(bf16[4,9,16,2,8,12]{5,4,2,3,1,0:T(8,128)(2,1)} %fusion.2) | data formatting | bytes 442368 | tf_op jit(solution)/shard_map/conv_general_dilated | solution.py:27
  26.1 2.4 %copy.138 = bf16[4,9,16,16,12]{3,0,4,2,1:T(4,128)(2,1)} copy(bf16[4,9,16,16,12]{2,3,4,1,0:T(8,128)(2,1)S(1)} %bitcast.103) | data formatting | bytes 442368 | tf_op jit(solution)/shard_map/conv_general_dilated | solution.py:27
  28.5 4.7 %multiply_convert_fusion = (bf16[4,8,16,5,32]{4,2,3,1,0:T(8,128)(2,1)S(1)}, f32[4,8,16,5,32]{4,2,3,1,0:T(8,128)}) fusion(bf16[4,9,16,16,12]{3,0,4,2,1:T(4,128)(2,1)} %copy.138, bf16[32,3,3,3,4]{0,4,3,2,1:T(4,128)(2,1)S(1)} %reshape.29, pred[16,5]{0,1:T(8,128)(4,1)S(1)} %copy-done.5), kind=kOutput, calls=%fused_computation.14 | convolution fusion | flops 17776640 | bytes 719696 | tf_op jit(solution)/shard_map/conv_general_dilated | solution.py:27
  33.3 0.1 copy.202
  33.4 4.2 %collective-permute-start.1 = (bf16[2,32,1,8,32]{1,0,4,3,2:T(2,128)(2,1)S(1)}, bf16[2,32,1,8,32]{1,0,4,3,2:T(2,128)(2,1)S(1)}, u32[]{:S(2)}, u32[]{:S(2)}) collective-permute-start(bf16[2,32,1,8,32]{1,0,4,3,2:T(2,128)(2,1)S(1)} %bitcast.129), channel_id=1, source_target_pairs={{0,1},{2,3},{4,5},{6,7},{8,9},{10,11},{12,13},{14,15},{16,17},{18,... | collective-permute-start | bytes 98312 | tf_op jit(solution)/shard_map/ppermute | solution.py:14
  37.7 0.2 copy.145
  37.9 0.2 copy.141
  38.1 0.5 copy.201
  38.6 1.5 collective-permute-done.1
  40.2 1.0 fusion.55
  41.2 0.9 pad.2
  42.1 0.2 copy.144
  42.4 0.3 copy-done.7
  42.7 0.8 multiply_convert_fusion.1
  43.7 0.7 reshape.101
  44.4 3.7 %all-to-all-start = ((bf16[2,2,4096]{2,1,0:T(2,128)(2,1)}), bf16[2,2,4096]{2,1,0:T(2,128)(2,1)S(1)}, u32[]{:S(2)}, u32[]{:S(2)}) async-start(bf16[2,2,4096]{2,1,0:T(2,128)(2,1)} %reshape.101), calls=%async_computation | async-start | bytes 65536 | tf_op jit(solution)/shard_map/all_to_all | solution.py:89
  48.1 8.6 %copy.165 = bf16[2,4,9,16,64]{1,0,4,3,2:T(2,128)(2,1)} copy(bf16[2,4,9,16,64]{4,3,2,1,0:T(8,128)(2,1)S(1)} %constant_dynamic-update-slice_fusion) | data formatting | bytes 294912 | tf_op jit(solution)/shard_map/concatenate | solution.py:82
  56.8 1.7 copy.164
  58.6 0.1 reshape.102
  58.9 0.6 add_multiply_fusion.1
  59.7 0.8 fusion.10
  60.7 0.7 reshape.103
  61.5 3.5 %all-to-all-start.1 = ((bf16[2,2,4096]{2,1,0:T(2,128)(2,1)}), bf16[2,2,4096]{2,1,0:T(2,128)(2,1)S(1)}, u32[]{:S(2)}, u32[]{:S(2)}) async-start(bf16[2,2,4096]{2,1,0:T(2,128)(2,1)} %reshape.103), calls=%async_computation.1 | async-start | bytes 65536 | tf_op jit(solution)/shard_map/all_to_all | solution.py:97
  64.9 2.5 %fusion.39 = f32[128,3,3,3,64]{0,4,3,2,1:T(8,128)} fusion(bf16[1,128,4,4,16]{1,3,4,2,0:T(4,128)(2,1)S(1)} %fusion.36, bf16[1,64,4,4,16]{1,4,3,2,0:T(8,128)(2,1)S(1)} %bitcast.113), kind=kOutput, calls=%fused_computation.57 | convolution fusion | flops 75366400 | bytes 983040 | tf_op jit(solution)/shard_map/transpose | solution.py:23
  67.5 1.4 all-to-all-done.1
  69.0 1.3 collective-permute-start.2
  70.3 1.6 fusion.44
  71.9 0.9 copy.168
  72.8 2.0 collective-permute-done.2
  75.0 0.1 pad.8.clone
  75.2 0.2 fusion.20
  75.4 0.8 convolution_select_fusion
  76.2 0.9 copy.163
  77.3 11.5 %fusion.16 = f32[32,3,3,3,4]{0,4,3,2,1:T(4,128)S(1)} fusion(bf16[2,4,9,16,64]{1,0,4,3,2:T(2,128)(2,1)} %copy.165, bf16[4,8,2,32,32]{4,1,3,2,0:T(8,128)(2,1)S(1)} %fusion.14), kind=kOutput, calls=%fused_computation.26 | convolution fusion | flops 13424640 | bytes 292352 | tf_op jit(solution)/shard_map/transpose | solution.py:23
  88.8 40.3 %psum.21 = f32[32,108]{0,1:T(8,128)S(1)} all-reduce(f32[32,108]{0,1:T(8,128)S(1)} %reshape.32), channel_id=1, replica_groups=mesh['vol'=16,'slab'=2] {'vol','slab'}, use_global_device_ids=true, to_apply=%region_0.1 | all-reduce | flops 3456 | bytes 27648 | tf_op jit(solution)/shard_map/psum | solution.py:109
  129.2 0.7 copy.171
  129.9 76.0 %all-reduce.3.cloned.1.call-done = (f32[64,864]{1,0:T(8,128)}, f32[128,1728]{0,1:T(8,128)}) async-done(((f32[64,864]{1,0:T(8,128)}, f32[128,1728]{0,1:T(8,128)}), (f32[64,864]{1,0:T(8,128)}, f32[128,1728]{0,1:T(8,128)})) %all-reduce.3.cloned.1.call-update) | async-done | bytes 1105936 | tf_op jit(solution)/shard_map/psum | solution.py:109
  205.9 2.2 %broadcast_multiply_fusion = f32[128,1728]{0,1:T(8,128)} fusion(f32[128,1728]{0,1:T(8,128)} %get-tuple-element.16), kind=kLoop, calls=%fused_computation.28 | loop fusion | flops 221184 | bytes 1769472 | tf_op jit(solution)/shard_map/mul | solution.py:113
  208.1 0.7 broadcast_multiply_fusion.1
  (56 shorter events, 1.3 us)
Async XLA Ops:
  7.2 51.7 %copy-start = (bf16[128,1728]{0,1:T(8,128)(2,1)S(1)}, bf16[128,1728]{0,1:T(8,128)(2,1)}, u32[]{:S(2)}) copy-start(bf16[128,1728]{0,1:T(8,128)(2,1)} %param.8) | copy-start | bytes 1327108
  8.0 6.4 %collective-permute-start = (bf16[2,4,1,16,64]{4,3,2,1,0:T(8,128)(2,1)S(1)}, bf16[2,4,1,16,64]{4,3,2,1,0:T(8,128)(2,1)S(1)}, u32[]{:S(2)}, u32[]{:S(2)}) collective-permute-start(bf16[2,4,1,16,64]{4,3,2,1,0:T(8,128)(2,1)S(1)} %slice.15), channel_id=1, source_target_pairs={{0,1},{2,3},{4,5},{6,7},{8,9},{10,11},{12,13},{14,15},{16,17},{18,... | collective-permute-start | bytes 49160 | tf_op jit(solution)/shard_map/ppermute | solution.py:14
  26.1 2.4 %copy-start.5 = (pred[16,5]{0,1:T(8,128)(4,1)S(1)}, pred[16,5]{0,1:T(8,128)(4,1)}, u32[]{:S(2)}) copy-start(pred[16,5]{0,1:T(8,128)(4,1)} %constant.38) | copy-start | bytes 244
  28.5 9.2 %copy-start.2 = (bf16[64,864]{1,0:T(8,128)(2,1)S(1)}, bf16[64,864]{1,0:T(8,128)(2,1)}, u32[]{:S(2)}) copy-start(bf16[64,864]{1,0:T(8,128)(2,1)} %param.7) | copy-start | bytes 331780
  33.4 6.7 %collective-permute-start.1 = (bf16[2,32,1,8,32]{1,0,4,3,2:T(2,128)(2,1)S(1)}, bf16[2,32,1,8,32]{1,0,4,3,2:T(2,128)(2,1)S(1)}, u32[]{:S(2)}, u32[]{:S(2)}) collective-permute-start(bf16[2,32,1,8,32]{1,0,4,3,2:T(2,128)(2,1)S(1)} %bitcast.129), channel_id=1, source_target_pairs={{0,1},{2,3},{4,5},{6,7},{8,9},{10,11},{12,13},{14,15},{16,17},{18,... | collective-permute-start | bytes 98312 | tf_op jit(solution)/shard_map/ppermute | solution.py:14
  42.1 0.7 copy-start.7
  44.4 14.2 %all-to-all-start = ((bf16[2,2,4096]{2,1,0:T(2,128)(2,1)}), bf16[2,2,4096]{2,1,0:T(2,128)(2,1)S(1)}, u32[]{:S(2)}, u32[]{:S(2)}) async-start(bf16[2,2,4096]{2,1,0:T(2,128)(2,1)} %reshape.101), calls=%async_computation | async-start | bytes 65536 | tf_op jit(solution)/shard_map/all_to_all | solution.py:89
  56.8 2.1 copy-start.6
  58.6 1.0 copy-start.3
  61.5 7.4 %all-to-all-start.1 = ((bf16[2,2,4096]{2,1,0:T(2,128)(2,1)}), bf16[2,2,4096]{2,1,0:T(2,128)(2,1)S(1)}, u32[]{:S(2)}, u32[]{:S(2)}) async-start(bf16[2,2,4096]{2,1,0:T(2,128)(2,1)} %reshape.103), calls=%async_computation.1 | async-start | bytes 65536 | tf_op jit(solution)/shard_map/all_to_all | solution.py:97
  64.9 141.0 %all-reduce.3.cloned.1.call-start = ((), (), s32[]{:S(2)}) async-start(), calls=%async_computation.2 | async-start | bytes 2228224 | tf_op jit(solution)/shard_map/psum | solution.py:109
  69.0 5.8 %collective-permute-start.2 = (bf16[2,64,1,4,16]{1,4,3,2,0:T(8,128)(2,1)S(1)}, bf16[2,64,1,4,16]{1,4,3,2,0:T(8,128)(2,1)S(1)}, u32[]{:S(2)}, u32[]{:S(2)}) collective-permute-start(bf16[2,64,1,4,16]{1,4,3,2,0:T(8,128)(2,1)S(1)} %slice.51), channel_id=1, source_target_pairs={{1,0},{3,2},{5,4},{7,6},{9,8},{11,10},{13,12},{15,14},{17,16},{19,... | collective-permute-start | bytes 49160 | tf_op jit(solution)/shard_map/ppermute | solution.py:14
  71.9 3.5 %copy-start.4 = (pred[16,6]{0,1:T(8,128)(4,1)S(1)}, pred[16,6]{0,1:T(8,128)(4,1)}, u32[]{:S(2)}) copy-start(pred[16,6]{0,1:T(8,128)(4,1)} %constant.34) | copy-start | bytes 292
  205.9 2.2 %copy-start.1 = (f32[64,864]{1,0:T(8,128)S(1)}, f32[64,864]{1,0:T(8,128)}, u32[]{:S(2)}) copy-start(f32[64,864]{1,0:T(8,128)} %get-tuple-element.15) | copy-start | bytes 663556
Sparse Core Ops, SparseCore 0:
  72.9 132.9 all-reduce.2
